TPU v7x, 512 devices: a whole 4x4x16 slice. The times are simulated.
512 devices in a mesh: group: 4 (over x), shard: 32 (over z, y_hi), tensor: 4 (over y_lo, core).
Axes of the slice: x: 4, y: 4 (y_hi: 2, y_lo: 2; y = y_hi * 2 + y_lo), z: 16, core: 2. Of those that a mesh axis runs over, the one named last changes fastest.
Arguments:
- deltas: bfloat16 [4, 2048, 2048], P('group', None, 'tensor'), may hold values from -6 to 6
- factor: bfloat16 [2048, 64], P('tensor'), may hold values from -0.29882812 to 0.29882812
- master: float32 [2048, 2048], P(('group', 'shard'), 'tensor'), may hold values from -6 to 6
- momentum: float32 [2048, 2048], P(('group', 'shard'), 'tensor'), may hold values from -3 to 3
Outputs:
- new_master: float32 [2048, 2048], P(('group', 'shard'), 'tensor')
- new_momentum: float32 [2048, 2048], P(('group', 'shard'), 'tensor')
- weights: bfloat16 [2048, 2048], P(None, 'tensor')
All inputs are finite; a program needn't handle non-finite values.
Results may differ from a plain program's by a relative error of at most 0.009.
Values may be sent and summed in bfloat16 or wider, within the bound.
A program may use at most 64 MiB of HBM per device.

v0:
```python
import jax
import jax.numpy as jnp
from jax import lax
from jax.sharding import PartitionSpec as P

momentum_rate = 0.9
outer_rate = 0.7


def shards(deltas, factor, master, momentum):
    group_count = lax.axis_size("group")
    shard_count = lax.axis_size("shard")
    shard_index = lax.axis_index("shard")
    row_count = master.shape[0]
    col_count = master.shape[1]
    own_delta = deltas[0]
    blocks = own_delta.reshape(group_count, shard_count, row_count, col_count)
    picked = lax.dynamic_index_in_dim(blocks, shard_index, 1, keepdims=False)
    factor_wide = factor.astype(jnp.float32)
    summed = lax.psum_scatter(
        picked.astype(jnp.float32).astype(jnp.bfloat16), "group", scatter_dimension=0, tiled=True
    ).astype(jnp.float32)
    partial_value = jnp.dot(summed[0], factor_wide, precision=lax.Precision.HIGHEST)
    coefficients = lax.psum(partial_value, "tensor")
    outer_grad = (
        lax.dot_general(
            coefficients, factor_wide, (((1,), (1,)), ((), ())), precision=lax.Precision.HIGHEST
        )
        / group_count
    )
    new_momentum = momentum_rate * momentum + outer_grad
    new_master = master - outer_rate * (outer_grad + momentum_rate * new_momentum)
    fresh_copy = new_master.astype(jnp.bfloat16)
    weights = lax.all_gather(fresh_copy, ("group", "shard"), axis=0, tiled=True)
    return (new_master, new_momentum, weights)


def solution(mesh):
    return jax.shard_map(
        shards,
        mesh=mesh,
        in_specs=(
            P("group", None, "tensor"),
            P("tensor", None),
            P(("group", "shard"), "tensor"),
            P(("group", "shard"), "tensor"),
        ),
        out_specs=(
            P(("group", "shard"), "tensor"),
            P(("group", "shard"), "tensor"),
            P(None, "tensor"),
        ),
        check_vma=False,
    )
```

profile of v0, /device:TPU:6, one launch (start us, length us, event | category | flops | bytes accessed | tf_op | source)
XLA Modules:
  0.0 274.1 jit_solution(17234697237845103731)
XLA Ops:
  7.2 0.0 copy-start
  7.2 0.0 reduce-scatter.2.cloned.1.call-start
  7.2 1.5 copy-done
  8.8 0.6 dynamic-slice_bitcast_fusion
  9.4 0.0 reduce-scatter.2.cloned.1.call-update
  9.4 0.0 all-gather.2.cloned.1.call-start
  9.5 33.2 %reduce-scatter.2.cloned.1.call-done = bf16[1,16,512]{2,1,0:T(8,128)(2,1)} async-done(((bf16[4,16,512]{2,1,0:T(8,128)(2,1)}), bf16[1,16,512]{2,1,0:T(8,128)(2,1)}) %reduce-scatter.2.cloned.1.call-update) | async-done | bytes 16400 | tf_op jit(solution)/shard_map/reduce_scatter | solution.py:20
  42.6 1.0 fusion
  43.6 5.7 %psum.7 = f32[16,64]{1,0:T(8,128)S(1)} all-reduce(f32[16,64]{1,0:T(8,128)S(1)} %fusion), channel_id=1, replica_groups=mesh['group'=4,'shard'=32,'tensor'=4] {'tensor'}, use_global_device_ids=true, to_apply=%region_1.2 | all-reduce | flops 1024 | bytes 8192 | tf_op jit(solution)/shard_map/psum | solution.py:24
  49.4 1.6 fusion.2
  51.0 0.0 all-gather.2.cloned.1.call-update
  51.0 213.1 %all-gather.2.cloned.1.call-done = bf16[2048,512]{1,0:T(8,128)(2,1)} async-done(((bf16[16,512]{1,0:T(8,128)(2,1)}), bf16[2048,512]{1,0:T(8,128)(2,1)}) %all-gather.2.cloned.1.call-update) | async-done | bytes 2097168 | tf_op jit(solution)/shard_map/all_gather | solution.py:34
  264.2 3.0 %copy.8 = bf16[2048,512]{1,0:T(8,128)(2,1)} copy(bf16[2048,512]{1,0:T(8,128)(2,1)} %all-gather.2.cloned.1.call-done) | data formatting | bytes 4194304
Async XLA Ops:
  7.2 1.6 copy-start
  7.2 35.5 %reduce-scatter.2.cloned.1.call-start = ((), (), s32[]{:S(2)}) async-start(), calls=%async_computation.1 | async-start | bytes 81920 | tf_op jit(solution)/shard_map/reduce_scatter | solution.py:20
  9.4 254.8 %all-gather.2.cloned.1.call-start = ((), (), s32[]{:S(2)}) async-start(), calls=%async_computation.2 | async-start | bytes 2113536 | tf_op jit(solution)/shard_map/all_gather | solution.py:34
Sparse Core Ops, SparseCore 0:
  11.4 31.2 reduce-scatter.1
  51.2 212.9 all-gather.1
where the time goes:
time: 274 us
  waiting for transfers between devices  246 us (90%)
  between operations  14.1 us (5%)
  blocking collectives  5.75 us (2%)
  local copies, waits for them, and re-layouts  5.22 us (2%)
    all_gather x1, waiting for transfers between devices, shards(): weights = lax.all_gather(fresh_copy, ('group', 'shard'), axis=0, tiled=True)  213 us
    reduce_scatter x1, waiting for transfers between devices, shards(): lax.psum_scatter(picked.astype(jnp.float32).astype(jnp.bfloat16), 'group'...  33.2 us
    psum x1, blocking collectives, shards(): coefficients = lax.psum(partial_value, 'tensor')  5.75 us
  transfers between devices with their start and end apart: 2, of which 2 were waited for; matrix products, arithmetic and copies ran while one was open for 0% of the time, Pallas kernels for 0%

commit v1 on v0

v1 whole, which is shorter than its diff:
```python
import jax
import jax.numpy as jnp
from jax import lax
from jax.experimental import pallas as pl
from jax.experimental.pallas import tpu as pltpu
from jax.sharding import PartitionSpec as P

momentum_rate = 0.9
outer_rate = 0.7
MESH = pl.DeviceIdType.MESH


def kernel(
    deltas_ref, factor_ref, master_ref, momentum_ref,
    new_master_ref, new_momentum_ref, weights_ref,
    delta, factor, master, momentum, partial, incoming, new_master, new_momentum, full,
    in_sem, out_sem, full_sem, sum_send, sum_recv, plane_send, plane_recv, ring_send, ring_recv,
):
    groups, depth = full.shape[0], full.shape[1]
    tensors = lax.axis_size("tensor")
    g, s, t = lax.axis_index("group"), lax.axis_index("shard"), lax.axis_index("tensor")
    z, y = s // 2, s % 2
    rows = master.shape[0]
    half = rows // 2
    rank = factor.shape[0]

    loads = [
        pltpu.make_async_copy(deltas_ref.at[:, s], delta, in_sem.at[0]),
        pltpu.make_async_copy(factor_ref, factor, in_sem.at[1]),
        pltpu.make_async_copy(master_ref, master, in_sem.at[2]),
        pltpu.make_async_copy(momentum_ref, momentum, in_sem.at[3]),
    ]
    for load in loads:
        load.start()

    def around(value, step, size):
        return lax.rem(value + step + size, size)

    def device(dg, dy, dz, dt):
        shard = around(z, dz, depth) * 2 + around(y, dy, 2)
        return (around(g, dg, groups), shard, around(t, dt, tensors))

    sums = [(dg, dt) for dg in range(groups) for dt in range(tensors) if dg or dt]
    planes = [(dg, dy) for dg in range(groups) for dy in range(2) if dg or dy]
    peers = [(dg, 0, 0, dt) for dg, dt in sums]
    peers += [(dg, 1, 0, 0) for dg in range(groups)]
    peers += [(0, 0, 1, 0), (0, 0, -1, 0)]
    barrier = pltpu.get_barrier_semaphore()
    for peer in peers:
        pl.semaphore_signal(barrier, inc=1, device_id=device(*peer), device_id_type=MESH)

    loads[0].wait()
    loads[1].wait()
    part = lax.dot_general(
        delta[...].reshape(groups * rows, delta.shape[2]), factor[...], (((1,), (1,)), ((), ())),
        preferred_element_type=jnp.float32,
    )
    for i in range(groups):
        partial[i] = jnp.concatenate(
            [part[i * rows : i * rows + half], part[i * rows + half : (i + 1) * rows]], axis=1
        )

    pl.semaphore_wait(barrier, len(peers))

    copies = []
    for i, (dg, dt) in enumerate(sums):
        target = device(dg, 0, 0, dt)
        copy = pltpu.make_async_remote_copy(
            src_ref=partial.at[target[0]], dst_ref=incoming.at[i],
            send_sem=sum_send.at[i], recv_sem=sum_recv.at[i],
            device_id=target, device_id_type=MESH,
        )
        copy.start()
        copies.append(copy)
    loads[2].wait()
    loads[3].wait()
    total = partial[g]
    for i, copy in enumerate(copies):
        copy.wait_recv()
        total = total + incoming[i]
    coefficients = jnp.concatenate([total[:, :rank], total[:, rank:]], axis=0)
    outer_grad = lax.dot_general(
        coefficients, factor[...].astype(jnp.float32), (((1,), (0,)), ((), ())),
        precision=lax.Precision.HIGHEST, preferred_element_type=jnp.float32,
    ) / groups
    moved = momentum_rate * momentum[...] + outer_grad
    updated = master[...] - outer_rate * (outer_grad + momentum_rate * moved)
    fresh = updated.astype(jnp.bfloat16)
    full[g, z, y] = fresh

    plane_copies = {}
    for i, (dg, dy) in enumerate(planes):
        copy = pltpu.make_async_remote_copy(
            src_ref=full.at[g, z, y], dst_ref=full.at[g, z, y],
            send_sem=plane_send.at[i], recv_sem=plane_recv.at[i],
            device_id=device(dg, dy, 0, 0), device_id_type=MESH,
        )
        copy.start()
        plane_copies[dg, dy] = copy
    new_momentum[...] = moved
    new_master[...] = updated
    stores = [
        pltpu.make_async_copy(new_master, new_master_ref, out_sem.at[0]),
        pltpu.make_async_copy(new_momentum, new_momentum_ref, out_sem.at[1]),
    ]
    for store in stores:
        store.start()

    ring_copies = []

    def send(way, k, dg, block):
        copy = pltpu.make_async_remote_copy(
            src_ref=block, dst_ref=block,
            send_sem=ring_send.at[way, k, dg], recv_sem=ring_recv.at[way, k, dg],
            device_id=device(0, 0, 1 - 2 * way, 0), device_id_type=MESH,
        )
        copy.start()
        ring_copies.append(copy)

    def keep(block, g_of, z_of):
        pltpu.make_async_copy(block, weights_ref.at[g_of, z_of], full_sem).start()

    steps = depth // 2

    def last(way, dg):
        return (dg < groups // 2) == (way == 0)

    for dg in range(groups):
        g_of = around(g, -dg, groups)
        for dy in range(2):
            if dg or dy:
                plane_copies[dg, dy].wait_recv()
        block = full.at[g_of, z]
        for way in range(2):
            send(way, 0, dg, block)
        keep(block, g_of, z)
    for k in range(1, steps + 1):
        for dg in range(groups):
            g_of = around(g, -dg, groups)
            for way in range(2):
                if k == steps and not last(way, dg):
                    continue
                z_of = around(z, k if way else -k, depth)
                block = full.at[g_of, z_of]
                pltpu.make_async_remote_copy(
                    src_ref=block, dst_ref=block,
                    send_sem=ring_send.at[way, k - 1, dg], recv_sem=ring_recv.at[way, k - 1, dg],
                    device_id=device(0, 0, 1 - 2 * way, 0), device_id_type=MESH,
                ).wait_recv()
                if k < steps - 1 or (k == steps - 1 and last(way, dg)):
                    send(way, k, dg, block)
                keep(block, g_of, z_of)

    for copy in copies:
        copy.wait_send()
    for copy in plane_copies.values():
        copy.wait_send()
    for copy in ring_copies:
        copy.wait_send()
    for store in stores:
        store.wait()
    pltpu.make_async_copy(full, weights_ref, full_sem).wait()


def shards(deltas, factor, master, momentum):
    groups = lax.axis_size("group")
    tensors = lax.axis_size("tensor")
    depth = lax.axis_size("shard") // 2
    rows, cols = master.shape
    rank = factor.shape[1]
    steps = depth // 2
    hbm = pl.BlockSpec(memory_space=pl.ANY)
    dma = pltpu.SemaphoreType.DMA
    full = (groups, depth, 2, rows, cols)
    new_master, new_momentum, weights = pl.pallas_call(
        kernel,
        out_shape=(
            jax.ShapeDtypeStruct(master.shape, jnp.float32),
            jax.ShapeDtypeStruct(momentum.shape, jnp.float32),
            jax.ShapeDtypeStruct(full, jnp.bfloat16),
        ),
        in_specs=[hbm] * 4,
        out_specs=(hbm,) * 3,
        scratch_shapes=[
            pltpu.VMEM((groups, rows, cols), jnp.bfloat16),
            pltpu.VMEM((rank, cols), jnp.bfloat16),
            pltpu.VMEM((rows, cols), jnp.float32),
            pltpu.VMEM((rows, cols), jnp.float32),
            pltpu.VMEM((groups, rows // 2, 2 * rank), jnp.float32),
            pltpu.VMEM((groups * tensors - 1, rows // 2, 2 * rank), jnp.float32),
            pltpu.VMEM((rows, cols), jnp.float32),
            pltpu.VMEM((rows, cols), jnp.float32),
            pltpu.VMEM(full, jnp.bfloat16),
            dma((4,)), dma((2,)), dma,
            dma((groups * tensors - 1,)), dma((groups * tensors - 1,)),
            dma((groups * 2 - 1,)), dma((groups * 2 - 1,)),
            dma((2, steps, groups)), dma((2, steps, groups)),
        ],
        compiler_params=pltpu.CompilerParams(collective_id=0, has_side_effects=True),
    )(deltas.reshape(groups, 2 * depth, rows, cols), factor.T, master, momentum)
    return new_master, new_momentum, weights.reshape(groups * depth * 2 * rows, cols)


def solution(mesh):
    return jax.shard_map(
        shards,
        mesh=mesh,
        in_specs=(
            P("group", None, "tensor"),
            P("tensor", None),
            P(("group", "shard"), "tensor"),
            P(("group", "shard"), "tensor"),
        ),
        out_specs=(
            P(("group", "shard"), "tensor"),
            P(("group", "shard"), "tensor"),
            P(None, "tensor"),
        ),
        check_vma=False,
    )
```

time: 274 us -> 58.8 us (0.21)
  waiting for transfers between devices: 246 us -> 0 us
  Pallas kernels: 0 us -> 51.5 us
  between operations: 14.1 us -> 0.64 us
  blocking collectives: 5.75 us -> 0 us
    all_gather x1 -> x0, waiting for transfers between devices: 213 us -> none  [shards(): weights = lax.all_gather(fresh_copy, ('group', 'shard'), axis=0, tiled=True)]
    pallas_call x0 -> x1, Pallas kernels: none -> 51.5 us  [shards(): pl.pallas_call(kernel, out_shape=(jax.ShapeDtypeStruct(master.shape, jnp....]
    reduce_scatter x1 -> x0, waiting for transfers between devices: 33.2 us -> none  [shards(): lax.psum_scatter(picked.astype(jnp.float32).astype(jnp.bfloat16), 'group'...]
    psum x1 -> x0, blocking collectives: 5.75 us -> none  [shards(): coefficients = lax.psum(partial_value, 'tensor')]
  transfers between devices with their start and end apart: 2 -> 0, of which waited for: 2 -> 0; matrix products, arithmetic and copies ran while one was open for 0% -> 0% of each run, Pallas kernels for 0% -> 0%
where the time goes in v1:
time: 58.8 us; the launch traced here: 57.9 us
  Pallas kernels  51.5 us (88%)
  local copies, waits for them, and re-layouts  5.79 us (10%)
  between operations  0.64 us (1%)
    pallas_call x1, Pallas kernels, shards(): pl.pallas_call(kernel, out_shape=(jax.ShapeDtypeStruct(master.shape, jnp....  51.5 us
    unnamed x3, local copies, waits for them, and re-layouts  5.79 us

profile of v1, /device:TPU:6, one launch (start us, length us, event | category | flops | bytes accessed | tf_op | source)
XLA Modules:
  0.0 57.9 jit_solution(18392339895841229220)
XLA Ops:
  0.6 51.5 %shard_map.67 = (f32[16,512]{1,0:T(8,128)}, f32[16,512]{1,0:T(8,128)}, bf16[4,16,2,16,512]{4,3,2,1,0:T(8,128)(2,1)}) custom-call(bf16[4,32,16,512]{3,2,1,0:T(8,128)(2,1)} %bitcast.3, bf16[64,512]{1,0:T(8,128)(2,1)} %bitcast.5, f32[16,512]{1,0:T(8,128)} %master_ref.1, f32[16,512]{1,0:T(8,128)} %momentum_ref.1), custom_call_target="tpu_custom_call" | custom-call | tf_op jit(solution)/shard_map/pallas_call | solution.py:175
  52.1 1.4 %copy.10 = f32[16,512]{1,0:T(8,128)} copy(f32[16,512]{1,0:T(8,128)} %get-tuple-element.12) | data formatting | bytes 65536
  53.5 1.4 %copy.11 = f32[16,512]{1,0:T(8,128)} copy(f32[16,512]{1,0:T(8,128)} %get-tuple-element.13) | data formatting | bytes 65536
  54.8 3.0 %copy.12 = bf16[2048,512]{1,0:T(8,128)(2,1)} copy(bf16[2048,512]{1,0:T(8,128)(2,1)} %bitcast.4) | data formatting | bytes 4194304

commit v2 on v1

v2 whole, which is shorter than its diff:
```python
import jax
import jax.numpy as jnp
from jax import lax
from jax.experimental import pallas as pl
from jax.experimental.pallas import tpu as pltpu
from jax.sharding import PartitionSpec as P

momentum_rate = 0.9
outer_rate = 0.7
MESH = pl.DeviceIdType.MESH
AROUND = (1, -1, 2)


def kernel(
    deltas_ref, factor_ref, master_ref, momentum_ref,
    new_master, new_momentum, full,
    delta, factor, master, momentum, partial, incoming,
    in_sem, sum_send, sum_recv, far_send, far_recv, y_send, y_recv,
    mid_send, mid_recv, last_send, last_recv, pass_send, pass_recv,
):
    groups, zhs, zls = full.shape[:3]
    tensors = lax.axis_size("tensor")
    g, s, t = lax.axis_index("group"), lax.axis_index("shard"), lax.axis_index("tensor")
    z, y = s // 2, s % 2
    depth = zhs * zls
    rows = master.shape[0]
    half = rows // 2
    rank = factor.shape[0]

    loads = [
        pltpu.make_async_copy(deltas_ref.at[:, s], delta, in_sem.at[0]),
        pltpu.make_async_copy(factor_ref, factor, in_sem.at[1]),
        pltpu.make_async_copy(master_ref, master, in_sem.at[2]),
        pltpu.make_async_copy(momentum_ref, momentum, in_sem.at[3]),
    ]
    for load in loads:
        load.start()

    def around(value, step, size):
        return lax.rem(value + step + size, size)

    def device(dg, dy, dz, dt):
        shard = around(z, dz, depth) * 2 + around(y, dy, 2)
        return (around(g, dg, groups), shard, around(t, dt, tensors))

    sums = [(dg, dt) for dg in range(groups) for dt in range(tensors) if dg or dt]
    peers = [(dg, 0, 0, dt) for dg, dt in sums] + [(0, 1, 0, 0)]
    peers += [(0, 0, dz, 0) for dz in (1, -1, 2, -2, zls, -zls, 2 * zls)]
    barrier = pltpu.get_barrier_semaphore()
    for peer in peers:
        pl.semaphore_signal(barrier, inc=1, device_id=device(*peer), device_id_type=MESH)

    loads[0].wait()
    loads[1].wait()
    part = lax.dot_general(
        delta[...].reshape(groups * rows, delta.shape[2]), factor[...], (((1,), (1,)), ((), ())),
        preferred_element_type=jnp.float32,
    )
    for i in range(groups):
        partial[i] = jnp.concatenate(
            [part[i * rows : i * rows + half], part[i * rows + half : (i + 1) * rows]], axis=1
        )

    pl.semaphore_wait(barrier, len(peers))

    sent = []

    def copy(block, send_sem, recv_sem, target, into=None):
        return pltpu.make_async_remote_copy(
            src_ref=block, dst_ref=block if into is None else into,
            send_sem=send_sem, recv_sem=recv_sem, device_id=target, device_id_type=MESH,
        )

    def send(*args):
        move = copy(*args)
        move.start()
        sent.append(move)

    for i, (dg, dt) in enumerate(sums):
        target = device(dg, 0, 0, dt)
        send(partial.at[target[0]], sum_send.at[i], sum_recv.at[i], target, incoming.at[i])
    loads[2].wait()
    loads[3].wait()
    total = partial[g]
    for i in range(len(sums)):
        sent[i].wait_recv()
        total = total + incoming[i]
    coefficients = jnp.concatenate([total[:, :rank], total[:, rank:]], axis=0)
    outer_grad = lax.dot_general(
        coefficients, factor[...].astype(jnp.float32), (((1,), (0,)), ((), ())),
        precision=lax.Precision.HIGHEST, preferred_element_type=jnp.float32,
    ) / groups
    moved = momentum_rate * momentum[...] + outer_grad
    updated = master[...] - outer_rate * (outer_grad + momentum_rate * moved)

    def places(z_of):
        zh, zl = z_of // zls, lax.rem(z_of, zls)
        return [zh] + [around(zh, -d, zhs) for d in AROUND], zl

    zh_mine, zl = places(z)
    here = full.at[g, zh_mine[0], zl, y]
    here[0] = updated[:half].astype(jnp.bfloat16)
    here[1] = updated[half:].astype(jnp.bfloat16)

    def far(i):
        return full.at[g, zh_mine[i], zl, y]

    def over_y(i):
        send(far(i), y_send.at[i], y_recv.at[i], device(0, 1, 0, 0))

    def wait(block, send_sem, recv_sem):
        copy(block, send_sem, recv_sem, device(0, 1, 0, 0)).wait_recv()

    for i, d in enumerate(AROUND):
        send(here, far_send.at[i], far_recv.at[i], device(0, 0, d * zls, 0))
    over_y(0)
    new_momentum[...] = moved
    new_master[...] = updated

    def hop(axis, d):
        return device(d, 0, 0, 0) if axis == 0 else device(0, 0, d, 0)

    def mid(i):
        wait(full.at[g, zh_mine[i], zl, 1 - y], y_send.at[i], y_recv.at[i])
        for part in range(2):
            block = full.at[g, zh_mine[i], zl, :, part]
            for j, d in enumerate(AROUND):
                send(block, mid_send.at[part, j, i], mid_recv.at[part, j, i], hop(part, d))

    for i in range(1, 3):
        wait(far(i), far_send.at[i - 1], far_recv.at[i - 1])
        over_y(i)
    mid(0)
    wait(far(3), far_send.at[2], far_recv.at[2])
    over_y(3)
    for i in range(1, 4):
        mid(i)

    def chunk(part, u, w):
        if part == 0:
            return full.at[around(g, -u, groups), :, around(zl, -w, zls), :, 0]
        return full.at[around(g, -w, groups), :, around(zl, -u, zls), :, 1]

    froms = (0,) + AROUND
    for j, d in enumerate(froms):
        for part in range(2):
            if j:
                for i in range(4):
                    if part == 0:
                        block = full.at[around(g, -d, groups), zh_mine[i], zl, :, 0]
                    else:
                        zh_of, zl_of = places(around(z, -d, depth))
                        block = full.at[g, zh_of[i], zl_of, :, 1]
                    wait(block, mid_send.at[part, j - 1, i], mid_recv.at[part, j - 1, i])
            for way in range(2):
                send(
                    chunk(part, d, 0), last_send.at[part, way, j], last_recv.at[part, way, j],
                    hop(1 - part, 1 - 2 * way),
                )
    for j, d in enumerate(froms):
        for part in range(2):
            for way in range(2):
                block = chunk(part, d, 1 - 2 * way)
                wait(block, last_send.at[part, way, j], last_recv.at[part, way, j])
                if j % 2 == way:
                    send(block, pass_send.at[part, j], pass_recv.at[part, j], hop(1 - part, 1 - 2 * way))
    for j, d in enumerate(froms):
        for part in range(2):
            wait(chunk(part, d, 2), pass_send.at[part, j], pass_recv.at[part, j])
    for move in sent:
        move.wait_send()


def store(*refs):
    sem = refs[-1]
    count = len(refs) // 2
    moves = [pltpu.make_async_copy(refs[i], refs[count + i], sem.at[i]) for i in range(count)]
    for move in moves:
        move.start()
    for move in moves:
        move.wait()


def shards(deltas, factor, master, momentum):
    groups = lax.axis_size("group")
    tensors = lax.axis_size("tensor")
    depth = lax.axis_size("shard") // 2
    rows, cols = master.shape
    rank = factor.shape[1]
    anywhere = pl.BlockSpec(memory_space=pl.ANY)
    vmem = pl.BlockSpec(memory_space=pltpu.VMEM)
    dma = pltpu.SemaphoreType.DMA
    full = (groups, 4, depth // 4, 2, 2, rows // 2, cols)
    results = pl.pallas_call(
        kernel,
        out_shape=(
            pltpu.VMEM(master.shape, jnp.float32),
            pltpu.VMEM(momentum.shape, jnp.float32),
            pltpu.VMEM(full, jnp.bfloat16),
        ),
        in_specs=[anywhere] * 4,
        out_specs=(vmem,) * 3,
        scratch_shapes=[
            pltpu.VMEM((groups, rows, cols), jnp.bfloat16),
            pltpu.VMEM((rank, cols), jnp.bfloat16),
            pltpu.VMEM((rows, cols), jnp.float32),
            pltpu.VMEM((rows, cols), jnp.float32),
            pltpu.VMEM((groups, rows // 2, 2 * rank), jnp.float32),
            pltpu.VMEM((groups * tensors - 1, rows // 2, 2 * rank), jnp.float32),
            dma((4,)), dma((groups * tensors - 1,)), dma((groups * tensors - 1,)),
            dma((3,)), dma((3,)), dma((4,)), dma((4,)),
            dma((2, 3, 4)), dma((2, 3, 4)), dma((2, 2, 4)), dma((2, 2, 4)), dma((2, 4)), dma((2, 4)),
        ],
        compiler_params=pltpu.CompilerParams(collective_id=0, has_side_effects=True),
    )(deltas.reshape(groups, 2 * depth, rows, cols), factor.T, master, momentum)
    new_master, new_momentum, weights = pl.pallas_call(
        store,
        out_shape=tuple(jax.ShapeDtypeStruct(r.shape, r.dtype) for r in results),
        in_specs=[anywhere] * 3,
        out_specs=(anywhere,) * 3,
        scratch_shapes=[dma((3,))],
        compiler_params=pltpu.CompilerParams(vmem_limit_bytes=1 << 20),
    )(*results)
    return new_master, new_momentum, weights.reshape(groups * depth * 2 * rows, cols)


def solution(mesh):
    return jax.shard_map(
        shards,
        mesh=mesh,
        in_specs=(
            P("group", None, "tensor"),
            P("tensor", None),
            P(("group", "shard"), "tensor"),
            P(("group", "shard"), "tensor"),
        ),
        out_specs=(
            P(("group", "shard"), "tensor"),
            P(("group", "shard"), "tensor"),
            P(None, "tensor"),
        ),
        check_vma=False,
    )
```

time: 58.8 us -> 49 us (0.83); the launches traced: 57.9 us -> 48.8 us
  local copies, waits for them, and re-layouts: 5.79 us -> 0 us
  Pallas kernels: 51.5 us -> 48.1 us
    unnamed x3 -> x0, local copies, waits for them, and re-layouts: 5.79 us -> none
    pallas_call x1 -> x2, Pallas kernels: 51.5 us -> 48.1 us  [the longest x1 46.8 us: shards(): pl.pallas_call(kernel, out_shape=(pltpu.VMEM(master.shape, jnp.float32),...]
where the time goes in v2:
time: 49 us; the launch traced here: 48.8 us
  Pallas kernels  48.1 us (98%)
  between operations  0.64 us (1%)
    pallas_call x1, Pallas kernels, shards(): pl.pallas_call(kernel, out_shape=(pltpu.VMEM(master.shape, jnp.float32),...  46.8 us
    pallas_call x1, Pallas kernels, shards(): pl.pallas_call(store, out_shape=tuple((jax.ShapeDtypeStruct(r.shape, r.dt...  1.37 us

profile of v2, /device:TPU:6, one launch (start us, length us, event | category | flops | bytes accessed | tf_op | source)
XLA Modules:
  0.0 48.8 jit_solution(9794495534370526180)
XLA Ops:
  0.6 46.8 %shard_map.67 = (f32[16,512]{1,0:T(8,128)S(1)}, f32[16,512]{1,0:T(8,128)S(1)}, bf16[4,4,4,2,2,8,512]{6,5,4,3,2,1,0:T(8,128)(2,1)S(1)}) custom-call(bf16[4,32,16,512]{3,2,1,0:T(8,128)(2,1)} %bitcast.3, bf16[64,512]{1,0:T(8,128)(2,1)} %bitcast.4, f32[16,512]{1,0:T(8,128)} %master_ref.1, f32[16,512]{1,0:T(8,128)} %momentum_ref.1), custom_call_target="tpu_custom_call" | custom-call | tf_op jit(solution)/shard_map/pallas_call | solution.py:194
  47.4 1.4 %shard_map.68 = (f32[16,512]{1,0:T(8,128)}, f32[16,512]{1,0:T(8,128)}, bf16[4,4,4,2,2,8,512]{6,5,4,3,2,1,0:T(8,128)(2,1)}) custom-call(f32[16,512]{1,0:T(8,128)S(1)} %get-tuple-element.9.refs_0_, f32[16,512]{1,0:T(8,128)S(1)} %get-tuple-element.10.refs_1_, bf16[4,4,4,2,2,8,512]{6,5,4,3,2,1,0:T(8,128)(2,1)S(1)} %get-tuple-element.11.refs_2_), custom_call_target="tpu_custom_call" | custom-call | tf_op jit(solution)/shard_map/pallas_call | solution.py:216

commit v3 on v2

v3 whole, which is shorter than its diff:
```python
import jax
import jax.numpy as jnp
from jax import lax
from jax.experimental import pallas as pl
from jax.experimental.pallas import tpu as pltpu
from jax.sharding import PartitionSpec as P

momentum_rate = 0.9
outer_rate = 0.7
MESH = pl.DeviceIdType.MESH
AROUND = (1, -1, 2)


def kernel(
    deltas_ref, factor_ref, master_ref, momentum_ref,
    new_master, new_momentum, full,
    delta, factor, master, momentum, partial, incoming, base, grad,
    in_sem, sum_send, sum_recv, far_send, far_recv, y_send, y_recv,
    mid_send, mid_recv, last_send, last_recv, pass_send, pass_recv,
):
    groups, zls = full.shape[0], full.shape[3]
    zhs = full.shape[1] * full.shape[2]
    tensors = lax.axis_size("tensor")
    g, s, t = lax.axis_index("group"), lax.axis_index("shard"), lax.axis_index("tensor")
    z, y = s // 2, s % 2
    depth = zhs * zls
    rows = master.shape[0]
    half = rows // 2
    rank = factor.shape[0]

    def around(value, step, size):
        return lax.rem(value + step + size, size)

    def device(dg, dy, dz, dt):
        shard = around(z, dz, depth) * 2 + around(y, dy, 2)
        return (around(g, dg, groups), shard, around(t, dt, tensors))

    def place(dz):
        other = around(z, dz, depth)
        return other // zls, lax.rem(other, zls)

    zh, zl = place(0)
    loads = [
        pltpu.make_async_copy(deltas_ref.at[:, :, zl, y], delta, in_sem.at[0]),
        pltpu.make_async_copy(factor_ref, factor, in_sem.at[1]),
        pltpu.make_async_copy(master_ref, master, in_sem.at[2]),
        pltpu.make_async_copy(momentum_ref, momentum, in_sem.at[3]),
    ]
    for load in loads:
        load.start()

    sums = [(dg, dt) for dg in range(groups) for dt in range(tensors) if dg or dt]
    peers = [(dg, 0, 0, dt) for dg, dt in sums] + [(0, 1, 0, 0)]
    peers += [(0, 0, dz, 0) for dz in (1, -1, 2, -2, zls, -zls)]
    barrier = pltpu.get_barrier_semaphore()
    for peer in peers:
        pl.semaphore_signal(barrier, inc=1, device_id=device(*peer), device_id_type=MESH)

    loads[2].wait()
    loads[3].wait()
    start = master[...] - outer_rate * momentum_rate * momentum_rate * momentum[...]
    mine = base.at[zh // 2, zh % 2]
    mine[0] = start[:half]
    mine[1] = start[half:]
    loads[0].wait()
    loads[1].wait()
    span = zhs * rows
    part = lax.dot_general(
        delta[...].reshape(groups * span, delta.shape[-1]), factor[...], (((1,), (1,)), ((), ())),
        preferred_element_type=jnp.float32,
    )
    for i in range(groups):
        own = part[i * span : (i + 1) * span]
        partial[i] = jnp.concatenate([own[: span // 2], own[span // 2 :]], axis=1)

    pl.semaphore_wait(barrier, len(peers))

    sent = []

    def copy(block, send_sem, recv_sem, target, into=None):
        return pltpu.make_async_remote_copy(
            src_ref=block, dst_ref=block if into is None else into,
            send_sem=send_sem, recv_sem=recv_sem, device_id=target, device_id_type=MESH,
        )

    def send(*args):
        move = copy(*args)
        move.start()
        sent.append(move)

    def wait(block, send_sem, recv_sem):
        copy(block, send_sem, recv_sem, device(0, 1, 0, 0)).wait_recv()

    def start_of(step):
        other = around(zh, step, zhs)
        return base.at[other // 2, other % 2]

    for way in range(2):
        send(mine, far_send.at[way], far_recv.at[way], device(0, 0, zls * (1 - 2 * way), 0))
    for i, (dg, dt) in enumerate(sums):
        target = device(dg, 0, 0, dt)
        send(partial.at[target[0]], sum_send.at[i], sum_recv.at[i], target, incoming.at[i])
    for way in range(2):
        block = start_of(2 * way - 1)
        wait(block, far_send.at[way], far_recv.at[way])
        send(
            block.at[way], far_send.at[2 + way], far_recv.at[2 + way],
            device(0, 0, zls * (1 - 2 * way), 0),
        )

    total = partial[g]
    for i in range(len(sums)):
        sent[2 + i].wait_recv()
        total = total + incoming[i]
    coefficients = jnp.concatenate([total[:, :rank], total[:, rank:]], axis=0)
    outer_grad = lax.dot_general(
        coefficients, factor[...].astype(jnp.float32), (((1,), (0,)), ((), ())),
        precision=lax.Precision.HIGHEST, preferred_element_type=jnp.float32,
    ) / groups
    grad[...] = outer_grad.reshape(grad.shape)

    def pair(k, dz=0):
        zh_of, zl_of = place(dz)
        return (zh_of + 1 - k) % 2, zl_of

    def finish(k):
        parity = pair(k)[0]
        fresh = base[:, parity] - outer_rate * (1 + momentum_rate) * grad[:, parity]
        full[g, :, parity, zl, y] = fresh.astype(jnp.bfloat16)
        send(full.at[g, :, parity, zl, y], y_send.at[k], y_recv.at[k], device(0, 1, 0, 0))

    def hop(axis, d):
        return device(d, 0, 0, 0) if axis == 0 else device(0, 0, d, 0)

    def block(part, u, w, k, o):
        dg, dz = (u, w) if part == 0 else (w, u)
        parity, zl_of = pair(k, -dz)
        return full.at[around(g, -dg, groups), :, parity, zl_of, y if o == 0 else 1 - y, part]

    froms = (0,) + AROUND

    def last(part, j, k, o):
        for way in range(2):
            send(
                block(part, froms[j], 0, k, o), last_send.at[part, way, j, k, o],
                last_recv.at[part, way, j, k, o], hop(1 - part, 1 - 2 * way),
            )

    def begin(k, o):
        if o:
            wait(full.at[g, :, pair(k)[0], zl, 1 - y], y_send.at[k], y_recv.at[k])
        for j, d in enumerate(AROUND):
            for part in range(2):
                send(
                    block(part, 0, 0, k, o), mid_send.at[part, j, k, o], mid_recv.at[part, j, k, o],
                    hop(part, d),
                )
        for part in range(2):
            last(part, 0, k, o)

    def middle(j, k, o):
        for part in range(2):
            wait(
                block(part, froms[j], 0, k, o), mid_send.at[part, j - 1, k, o], mid_recv.at[part, j - 1, k, o]
            )
            last(part, j, k, o)

    def onward(j, k, o):
        for part in range(2):
            for way in range(2):
                came = block(part, froms[j], 1 - 2 * way, k, o)
                wait(came, last_send.at[part, way, j, k, o], last_recv.at[part, way, j, k, o])
                if j % 2 == way:
                    send(
                        came, pass_send.at[part, j, k, o], pass_recv.at[part, j, k, o],
                        hop(1 - part, 1 - 2 * way),
                    )

    def ended(j, k, o):
        for part in range(2):
            came = block(part, froms[j], 2 - 4 * (j % 2), k, o)
            wait(came, pass_send.at[part, j, k, o], pass_recv.at[part, j, k, o])

    finish(0)
    begin(0, 0)
    moved = momentum_rate * momentum[...]
    own = grad.at[zh // 2, zh % 2]
    for i in range(2):
        new_momentum[i * half : (i + 1) * half] = moved[i * half : (i + 1) * half] + own[i]
        new_master[i * half : (i + 1) * half] = mine[i] - outer_rate * (1 + momentum_rate) * own[i]
    for j in (1, 2):
        middle(j, 0, 0)
    for way in range(2):
        wait(start_of(2).at[way], far_send.at[2 + way], far_recv.at[2 + way])
    finish(1)
    begin(1, 0)
    onward(0, 0, 0)
    begin(0, 1)
    middle(3, 0, 0)
    onward(1, 0, 0)
    onward(2, 0, 0)
    middle(1, 1, 0)
    middle(2, 1, 0)
    begin(1, 1)
    onward(0, 1, 0)
    middle(1, 0, 1)
    middle(2, 0, 1)
    onward(0, 0, 1)
    onward(3, 0, 0)
    middle(3, 1, 0)
    middle(3, 0, 1)
    onward(1, 1, 0)
    onward(2, 1, 0)
    middle(1, 1, 1)
    middle(2, 1, 1)
    onward(1, 0, 1)
    onward(2, 0, 1)
    onward(0, 1, 1)
    onward(3, 1, 0)
    onward(3, 0, 1)
    middle(3, 1, 1)
    onward(1, 1, 1)
    onward(2, 1, 1)
    onward(3, 1, 1)
    for o in range(2):
        for k in range(2):
            for j in range(4):
                ended(j, k, o)
    for move in sent:
        move.wait_send()


def store(*refs):
    sem = refs[-1]
    count = len(refs) // 2
    moves = [pltpu.make_async_copy(refs[i], refs[count + i], sem.at[i]) for i in range(count)]
    for move in moves:
        move.start()
    for move in moves:
        move.wait()


def shards(deltas, factor, master, momentum):
    groups = lax.axis_size("group")
    tensors = lax.axis_size("tensor")
    depth = lax.axis_size("shard") // 2
    rows, cols = master.shape
    rank = factor.shape[1]
    anywhere = pl.BlockSpec(memory_space=pl.ANY)
    vmem = pl.BlockSpec(memory_space=pltpu.VMEM)
    dma = pltpu.SemaphoreType.DMA
    zls = depth // 4
    full = (groups, 2, 2, zls, 2, 2, rows // 2, cols)
    four = (2, 2, 2, rows // 2, cols)
    results = pl.pallas_call(
        kernel,
        out_shape=(
            pltpu.VMEM(master.shape, jnp.float32),
            pltpu.VMEM(momentum.shape, jnp.float32),
            pltpu.VMEM(full, jnp.bfloat16),
        ),
        in_specs=[anywhere] * 4,
        out_specs=(vmem,) * 3,
        scratch_shapes=[
            pltpu.VMEM((groups, 4, rows, cols), jnp.bfloat16),
            pltpu.VMEM((rank, cols), jnp.bfloat16),
            pltpu.VMEM((rows, cols), jnp.float32),
            pltpu.VMEM((rows, cols), jnp.float32),
            pltpu.VMEM((groups, 2 * rows, 2 * rank), jnp.float32),
            pltpu.VMEM((groups * tensors - 1, 2 * rows, 2 * rank), jnp.float32),
            pltpu.VMEM(four, jnp.float32),
            pltpu.VMEM(four, jnp.float32),
            dma((4,)), dma((groups * tensors - 1,)), dma((groups * tensors - 1,)),
            dma((4,)), dma((4,)), dma((2,)), dma((2,)),
            dma((2, 3, 2, 2)), dma((2, 3, 2, 2)), dma((2, 2, 4, 2, 2)), dma((2, 2, 4, 2, 2)),
            dma((2, 4, 2, 2)), dma((2, 4, 2, 2)),
        ],
        compiler_params=pltpu.CompilerParams(collective_id=0, has_side_effects=True),
    )(deltas.reshape(groups, 4, zls, 2, rows, cols), factor.T, master, momentum)
    new_master, new_momentum, weights = pl.pallas_call(
        store,
        out_shape=tuple(jax.ShapeDtypeStruct(r.shape, r.dtype) for r in results),
        in_specs=[anywhere] * 3,
        out_specs=(anywhere,) * 3,
        scratch_shapes=[dma((3,))],
        compiler_params=pltpu.CompilerParams(vmem_limit_bytes=1 << 20),
    )(*results)
    return new_master, new_momentum, weights.reshape(groups * depth * 2 * rows, cols)


def solution(mesh):
    return jax.shard_map(
        shards,
        mesh=mesh,
        in_specs=(
            P("group", None, "tensor"),
            P("tensor", None),
            P(("group", "shard"), "tensor"),
            P(("group", "shard"), "tensor"),
        ),
        out_specs=(
            P(("group", "shard"), "tensor"),
            P(("group", "shard"), "tensor"),
            P(None, "tensor"),
        ),
        check_vma=False,
    )
```

time: 49 us -> 45.6 us (0.931)
  Pallas kernels: 48.1 us -> 44.5 us
    pallas_call x1, Pallas kernels: 46.8 us -> 43.1 us  [shards(): pl.pallas_call(kernel, out_shape=(pltpu.VMEM(master.shape, jnp.float32),...]
where the time goes in v3:
time: 45.6 us; the launch traced here: 45.1 us
  Pallas kernels  44.5 us (98%)
  between operations  0.64 us (1%)
    pallas_call x1, Pallas kernels, shards(): pl.pallas_call(kernel, out_shape=(pltpu.VMEM(master.shape, jnp.float32),...  43.1 us
    pallas_call x1, Pallas kernels, shards(): pl.pallas_call(store, out_shape=tuple((jax.ShapeDtypeStruct(r.shape, r.dt...  1.37 us

profile of v3, /device:TPU:6, one launch (start us, length us, event | category | flops | bytes accessed | tf_op | source)
XLA Modules:
  0.0 45.1 jit_solution(9620665944987556913)
XLA Ops:
  0.6 43.1 %shard_map.67 = (f32[16,512]{1,0:T(8,128)S(1)}, f32[16,512]{1,0:T(8,128)S(1)}, bf16[4,2,2,4,2,2,8,512]{7,6,5,4,3,2,1,0:T(8,128)(2,1)S(1)}) custom-call(bf16[4,4,4,2,16,512]{5,4,3,2,1,0:T(8,128)(2,1)} %bitcast.3, bf16[64,512]{1,0:T(8,128)(2,1)} %bitcast.4, f32[16,512]{1,0:T(8,128)} %master_ref.1, f32[16,512]{1,0:T(8,128)} %momentum_ref.1), custom_call_target="tpu_custom_call" | custom-call | tf_op jit(solution)/shard_map/pallas_call | solution.py:255
  43.8 1.4 %shard_map.68 = (f32[16,512]{1,0:T(8,128)}, f32[16,512]{1,0:T(8,128)}, bf16[4,2,2,4,2,2,8,512]{7,6,5,4,3,2,1,0:T(8,128)(2,1)}) custom-call(f32[16,512]{1,0:T(8,128)S(1)} %get-tuple-element.9.refs_0_, f32[16,512]{1,0:T(8,128)S(1)} %get-tuple-element.10.refs_1_, bf16[4,2,2,4,2,2,8,512]{7,6,5,4,3,2,1,0:T(8,128)(2,1)S(1)} %get-tuple-element.11.refs_2_), custom_call_target="tpu_custom_call" | custom-call | tf_op jit(solution)/shard_map/pallas_call | solution.py:280

commit v4 on v2

v4 whole, which is shorter than its diff:
```python
import jax
import jax.numpy as jnp
from jax import lax
from jax.experimental import pallas as pl
from jax.experimental.pallas import tpu as pltpu
from jax.sharding import PartitionSpec as P

momentum_rate = 0.9
outer_rate = 0.7
MESH = pl.DeviceIdType.MESH
AROUND = (1, -1, 2)


def kernel(
    deltas_ref, factor_ref, master_ref, momentum_ref,
    new_master, new_momentum, full,
    delta, factor, master, momentum, partial, incoming, base, grad,
    in_sem, sum_send, sum_recv, far_send, far_recv, y_send, y_recv,
    mid_send, mid_recv, last_send, last_recv, end_send, end_recv,
):
    groups, zhs, zls = full.shape[:3]
    tensors = lax.axis_size("tensor")
    g, s, t = lax.axis_index("group"), lax.axis_index("shard"), lax.axis_index("tensor")
    z, y = s // 2, s % 2
    depth = zhs * zls
    rows = master.shape[0]
    half = rows // 2
    rank = factor.shape[0]

    def around(value, step, size):
        return lax.rem(value + step + size, size)

    def device(dg, dy, dz, dt):
        shard = around(z, dz, depth) * 2 + around(y, dy, 2)
        return (around(g, dg, groups), shard, around(t, dt, tensors))

    zh, zl = z // zls, lax.rem(z, zls)
    loads = [
        pltpu.make_async_copy(master_ref, master, in_sem.at[0]),
        pltpu.make_async_copy(momentum_ref, momentum, in_sem.at[1]),
        pltpu.make_async_copy(deltas_ref.at[:, :, zl, y], delta, in_sem.at[2]),
        pltpu.make_async_copy(factor_ref, factor, in_sem.at[3]),
    ]
    for load in loads:
        load.start()

    sums = [(dg, dt) for dg in (2, 1, -1, 0) for dt in (2, 1, -1, 0) if dg or dt]
    peers = [(0, 0, dz, 0) for dz in (zls, -zls)]
    peers += [(0, dy, dz, 0) for dz in (2, -2, 1, -1) for dy in range(2)]
    peers += [(dg, 1, 0, 0) for dg in (2, 1, -1, 0)]
    peers += [(dg, 0, 0, dt) for dg, dt in sums]
    barrier = pltpu.get_barrier_semaphore()
    for peer in peers:
        pl.semaphore_signal(barrier, inc=1, device_id=device(*peer), device_id_type=MESH)

    loads[0].wait()
    loads[1].wait()
    start = master[...] - outer_rate * momentum_rate * momentum_rate * momentum[...]
    mine = base.at[zh]
    mine[0] = start[:half]
    mine[1] = start[half:]
    loads[2].wait()
    loads[3].wait()
    span = zhs * rows
    part = lax.dot_general(
        delta[...].reshape(groups * span, delta.shape[-1]), factor[...], (((1,), (1,)), ((), ())),
        preferred_element_type=jnp.float32,
    )
    for i in range(groups):
        own = part[i * span : (i + 1) * span]
        partial[i] = jnp.concatenate([own[: span // 2], own[span // 2 :]], axis=1)

    pl.semaphore_wait(barrier, len(peers))

    def copy(block, send_sem, recv_sem, target, into=None):
        return pltpu.make_async_remote_copy(
            src_ref=block, dst_ref=block if into is None else into,
            send_sem=send_sem, recv_sem=recv_sem, device_id=target, device_id_type=MESH,
        )

    def wait(block, send_sem, recv_sem):
        copy(block, send_sem, recv_sem, device(0, 1, 0, 0)).wait_recv()

    def wait_sent(block, send_sem):
        copy(block, send_sem, end_recv, device(0, 1, 0, 0)).wait_send()

    for way in range(2):
        copy(mine, far_send, far_recv.at[way], device(0, 0, zls * (1 - 2 * way), 0)).start()
    for i, (dg, dt) in enumerate(sums):
        target = device(dg, 0, 0, dt)
        copy(partial.at[target[0]], sum_send, sum_recv, target, incoming.at[i]).start()
    for way in range(2):
        block = base.at[around(zh, 2 * way - 1, zhs)]
        wait(block, far_send, far_recv.at[way])
        copy(
            block.at[way], far_send, far_recv.at[2 + way], device(0, 0, zls * (1 - 2 * way), 0)
        ).start()

    wait(incoming, sum_send, sum_recv)
    total = partial[g]
    for i in range(len(sums)):
        total = total + incoming[i]
    coefficients = jnp.concatenate([total[:, :rank], total[:, rank:]], axis=0)
    outer_grad = lax.dot_general(
        coefficients, factor[...].astype(jnp.float32), (((1,), (0,)), ((), ())),
        precision=lax.Precision.HIGHEST, preferred_element_type=jnp.float32,
    ) / groups
    grad[...] = outer_grad.reshape(grad.shape)
    for way in range(2):
        block = base.at[around(zh, 2, zhs), way]
        wait(block, far_send, far_recv.at[2 + way])
    fresh = base[...] - outer_rate * (1 + momentum_rate) * grad[...]
    full[g, :, zl, y] = fresh.astype(jnp.bfloat16)

    def hop(axis, d, dy=0):
        return device(d, dy, 0, 0) if axis == 0 else device(0, dy, d, 0)

    def block(part, u, w, o):
        dg, dz = (u, w) if part == 0 else (w, u)
        return full.at[around(g, -dg, groups), :, around(zl, -dz, zls), y if o == 0 else 1 - y, part]

    froms = (0,) + AROUND

    def last(part, j, o):
        for way in range(2):
            if j % 2 == way:
                came = last_recv.at[part, j, o]
            else:
                came = end_recv
            copy(block(part, froms[j], 0, o), last_send, came, hop(1 - part, 1 - 2 * way)).start()

    def middle(j, o):
        for part in range(2):
            wait(block(part, froms[j], 0, o), mid_send, mid_recv.at[part, j - 1, o])
            last(part, j, o)

    def onward(j, o):
        for part in range(2):
            way = j % 2
            came = block(part, froms[j], 1 - 2 * way, o)
            wait(came, last_send, last_recv.at[part, j, o])
            copy(came, end_send, end_recv, hop(1 - part, 1 - 2 * way)).start()

    for dy in range(2):
        if dy:
            here = full.at[g, :, zl, y]
            copy(here, y_send, y_recv, device(0, 1, 0, 0)).start()
        for j, d in enumerate(AROUND):
            for part in range(2):
                copy(block(part, 0, 0, 0), mid_send, mid_recv.at[part, j, dy], hop(part, d, dy)).start()
    for part in range(2):
        last(part, 0, 0)
    moved = momentum_rate * momentum[...]
    own = grad.at[zh]
    for i in range(2):
        new_momentum[i * half : (i + 1) * half] = moved[i * half : (i + 1) * half] + own[i]
        new_master[i * half : (i + 1) * half] = mine[i] - outer_rate * (1 + momentum_rate) * own[i]
    for j in range(1, 4):
        middle(j, 0)
    wait(full.at[g, :, zl, 1 - y], y_send, y_recv)
    for part in range(2):
        last(part, 0, 1)
    for j in range(1, 4):
        middle(j, 1)
    wait_sent(incoming, sum_send)
    wait_sent(base.at[0:3], far_send)
    wait_sent(full.at[0, :, 0, 0], y_send)
    for o in range(2):
        for j in range(4):
            onward(j, o)
    wait_sent(full.at[0:3, :, 0], mid_send)
    wait_sent(full.at[0:2], last_send)
    wait(full.at[0:2], end_send, end_recv)
    wait_sent(full.at[0:1], end_send)


def store(*refs):
    sem = refs[-1]
    count = len(refs) // 2
    moves = [pltpu.make_async_copy(refs[i], refs[count + i], sem.at[i]) for i in range(count)]
    for move in moves:
        move.start()
    for move in moves:
        move.wait()


def shards(deltas, factor, master, momentum):
    groups = lax.axis_size("group")
    tensors = lax.axis_size("tensor")
    depth = lax.axis_size("shard") // 2
    rows, cols = master.shape
    rank = factor.shape[1]
    anywhere = pl.BlockSpec(memory_space=pl.ANY)
    vmem = pl.BlockSpec(memory_space=pltpu.VMEM)
    dma = pltpu.SemaphoreType.DMA
    zls = depth // 4
    full = (groups, 4, zls, 2, 2, rows // 2, cols)
    four = (4, 2, rows // 2, cols)
    results = pl.pallas_call(
        kernel,
        out_shape=(
            pltpu.VMEM(master.shape, jnp.float32),
            pltpu.VMEM(momentum.shape, jnp.float32),
            pltpu.VMEM(full, jnp.bfloat16),
        ),
        in_specs=[anywhere] * 4,
        out_specs=(vmem,) * 3,
        scratch_shapes=[
            pltpu.VMEM((groups, 4, rows, cols), jnp.bfloat16),
            pltpu.VMEM((rank, cols), jnp.bfloat16),
            pltpu.VMEM((rows, cols), jnp.float32),
            pltpu.VMEM((rows, cols), jnp.float32),
            pltpu.VMEM((groups, 2 * rows, 2 * rank), jnp.float32),
            pltpu.VMEM((groups * tensors - 1, 2 * rows, 2 * rank), jnp.float32),
            pltpu.VMEM(four, jnp.float32),
            pltpu.VMEM(four, jnp.float32),
            dma((4,)), dma, dma, dma, dma((4,)), dma, dma,
            dma, dma((2, 3, 2)), dma, dma((2, 4, 2)), dma, dma,
        ],
        compiler_params=pltpu.CompilerParams(collective_id=0, has_side_effects=True),
    )(deltas.reshape(groups, 4, zls, 2, rows, cols), factor.T, master, momentum)
    new_master, new_momentum, weights = pl.pallas_call(
        store,
        out_shape=tuple(jax.ShapeDtypeStruct(r.shape, r.dtype) for r in results),
        in_specs=[anywhere] * 3,
        out_specs=(anywhere,) * 3,
        scratch_shapes=[dma((3,))],
        compiler_params=pltpu.CompilerParams(vmem_limit_bytes=1 << 20),
    )(*results)
    return new_master, new_momentum, weights.reshape(groups * depth * 2 * rows, cols)


def solution(mesh):
    return jax.shard_map(
        shards,
        mesh=mesh,
        in_specs=(
            P("group", None, "tensor"),
            P("tensor", None),
            P(("group", "shard"), "tensor"),
            P(("group", "shard"), "tensor"),
        ),
        out_specs=(
            P(("group", "shard"), "tensor"),
            P(("group", "shard"), "tensor"),
            P(None, "tensor"),
        ),
        check_vma=False,
    )
```

time: 49 us -> 42.2 us (0.86)
  Pallas kernels: 48.1 us -> 41.2 us
    pallas_call x1, Pallas kernels: 46.8 us -> 39.8 us  [shards(): pl.pallas_call(kernel, out_shape=(pltpu.VMEM(master.shape, jnp.float32),...]
where the time goes in v4:
time: 42.2 us; the launch traced here: 41.8 us
  Pallas kernels  41.2 us (98%)
  between operations  0.64 us (2%)
    pallas_call x1, Pallas kernels, shards(): pl.pallas_call(kernel, out_shape=(pltpu.VMEM(master.shape, jnp.float32),...  39.8 us
    pallas_call x1, Pallas kernels, shards(): pl.pallas_call(store, out_shape=tuple((jax.ShapeDtypeStruct(r.shape, r.dt...  1.37 us

profile of v4, /device:TPU:6, one launch (start us, length us, event | category | flops | bytes accessed | tf_op | source)
XLA Modules:
  0.0 41.8 jit_solution(4145481350837706440)
XLA Ops:
  0.6 39.8 %shard_map.67 = (f32[16,512]{1,0:T(8,128)S(1)}, f32[16,512]{1,0:T(8,128)S(1)}, bf16[4,4,4,2,2,8,512]{6,5,4,3,2,1,0:T(8,128)(2,1)S(1)}) custom-call(bf16[4,4,4,2,16,512]{5,4,3,2,1,0:T(8,128)(2,1)} %bitcast.3, bf16[64,512]{1,0:T(8,128)(2,1)} %bitcast.4, f32[16,512]{1,0:T(8,128)} %master_ref.1, f32[16,512]{1,0:T(8,128)} %momentum_ref.1), custom_call_target="tpu_custom_call" | custom-call | tf_op jit(solution)/shard_map/pallas_call | solution.py:199
  40.4 1.4 %shard_map.68 = (f32[16,512]{1,0:T(8,128)}, f32[16,512]{1,0:T(8,128)}, bf16[4,4,4,2,2,8,512]{6,5,4,3,2,1,0:T(8,128)(2,1)}) custom-call(f32[16,512]{1,0:T(8,128)S(1)} %get-tuple-element.9.refs_0_, f32[16,512]{1,0:T(8,128)S(1)} %get-tuple-element.10.refs_1_, bf16[4,4,4,2,2,8,512]{6,5,4,3,2,1,0:T(8,128)(2,1)S(1)} %get-tuple-element.11.refs_2_), custom_call_target="tpu_custom_call" | custom-call | tf_op jit(solution)/shard_map/pallas_call | solution.py:222

commit v5 on v4

--- a/solution.py
+++ b/solution.py
@@ -18,7 +18,8 @@
     in_sem, sum_send, sum_recv, far_send, far_recv, y_send, y_recv,
     mid_send, mid_recv, last_send, last_recv, end_send, end_recv,
 ):
-    groups, zhs, zls = full.shape[:3]
+    groups, zls = full.shape[0], full.shape[3]
+    zhs = full.shape[1] * full.shape[2]
     tensors = lax.axis_size("tensor")
     g, s, t = lax.axis_index("group"), lax.axis_index("shard"), lax.axis_index("tensor")
     z, y = s // 2, s % 2
@@ -34,7 +35,11 @@
         shard = around(z, dz, depth) * 2 + around(y, dy, 2)
         return (around(g, dg, groups), shard, around(t, dt, tensors))
 
-    zh, zl = z // zls, lax.rem(z, zls)
+    def place(dz):
+        other = around(z, dz, depth)
+        return other // zls, lax.rem(other, zls)
+
+    zh, zl = place(0)
     loads = [
         pltpu.make_async_copy(master_ref, master, in_sem.at[0]),
         pltpu.make_async_copy(momentum_ref, momentum, in_sem.at[1]),
@@ -56,7 +61,12 @@
     loads[0].wait()
     loads[1].wait()
     start = master[...] - outer_rate * momentum_rate * momentum_rate * momentum[...]
-    mine = base.at[zh]
+
+    def rows_of(ref, step):
+        other = around(zh, step, zhs)
+        return ref.at[other // 2, other % 2]
+
+    mine = rows_of(base, 0)
     mine[0] = start[:half]
     mine[1] = start[half:]
     loads[2].wait()
@@ -84,17 +94,22 @@
     def wait_sent(block, send_sem):
         copy(block, send_sem, end_recv, device(0, 1, 0, 0)).wait_send()
 
-    for way in range(2):
-        copy(mine, far_send, far_recv.at[way], device(0, 0, zls * (1 - 2 * way), 0)).start()
+    def far(way, order, part):
+        target = device(0, 0, zls * (1 - 2 * way), 0)
+        return copy(part, far_send, far_recv.at[way, order], target)
+
+    for order in range(2):
+        for way in range(2):
+            far(way, order, mine.at[(way + order) % 2]).start()
     for i, (dg, dt) in enumerate(sums):
         target = device(dg, 0, 0, dt)
         copy(partial.at[target[0]], sum_send, sum_recv, target, incoming.at[i]).start()
     for way in range(2):
-        block = base.at[around(zh, 2 * way - 1, zhs)]
-        wait(block, far_send, far_recv.at[way])
-        copy(
-            block.at[way], far_send, far_recv.at[2 + way], device(0, 0, zls * (1 - 2 * way), 0)
-        ).start()
+        came = rows_of(base, 2 * way - 1).at[way]
+        far(way, 0, came).wait_recv()
+        far(way, 2, came).start()
+    for way in range(2):
+        far(way, 1, rows_of(base, 2 * way - 1).at[1 - way]).wait_recv()
 
     wait(incoming, sum_send, sum_recv)
     total = partial[g]
@@ -106,69 +121,98 @@
         precision=lax.Precision.HIGHEST, preferred_element_type=jnp.float32,
     ) / groups
     grad[...] = outer_grad.reshape(grad.shape)
-    for way in range(2):
-        block = base.at[around(zh, 2, zhs), way]
-        wait(block, far_send, far_recv.at[2 + way])
-    fresh = base[...] - outer_rate * (1 + momentum_rate) * grad[...]
-    full[g, :, zl, y] = fresh.astype(jnp.bfloat16)
+
+    def pair(k, dz=0):
+        zh_of, zl_of = place(dz)
+        return (zh_of + 1 - k) % 2, zl_of
 
     def hop(axis, d, dy=0):
         return device(d, dy, 0, 0) if axis == 0 else device(0, dy, d, 0)
 
-    def block(part, u, w, o):
+    def block(part, u, w, k, o):
         dg, dz = (u, w) if part == 0 else (w, u)
-        return full.at[around(g, -dg, groups), :, around(zl, -dz, zls), y if o == 0 else 1 - y, part]
+        parity, zl_of = pair(k, -dz)
+        return full.at[around(g, -dg, groups), :, parity, zl_of, y if o == 0 else 1 - y, part]
 
     froms = (0,) + AROUND
 
-    def last(part, j, o):
+    def last(j, k, o, part):
         for way in range(2):
-            if j % 2 == way:
-                came = last_recv.at[part, j, o]
-            else:
-                came = end_recv
-            copy(block(part, froms[j], 0, o), last_send, came, hop(1 - part, 1 - 2 * way)).start()
-
-    def middle(j, o):
+            came = last_recv.at[part, j, k, o] if j % 2 == way else end_recv
+            copy(block(part, froms[j], 0, k, o), last_send, came, hop(1 - part, 1 - 2 * way)).start()
+
+    def finish(k):
+        parity = pair(k)[0]
+        fresh = base[:, parity] - outer_rate * (1 + momentum_rate) * grad[:, parity]
+        full[g, :, parity, zl, y] = fresh.astype(jnp.bfloat16)
+        for dy in range(2):
+            if dy:
+                here = full.at[g, :, parity, zl, y]
+                copy(here, y_send, y_recv.at[k], device(0, 1, 0, 0)).start()
+            for j, d in enumerate(AROUND):
+                for part in range(2):
+                    copy(
+                        block(part, 0, 0, k, 0), mid_send, mid_recv.at[part, j, k, dy], hop(part, d, dy)
+                    ).start()
         for part in range(2):
-            wait(block(part, froms[j], 0, o), mid_send, mid_recv.at[part, j - 1, o])
-            last(part, j, o)
-
-    def onward(j, o):
+            last(0, k, 0, part)
+
+    def middle(j, k, o):
+        for part in range(2):
+            if j:
+                wait(block(part, froms[j], 0, k, o), mid_send, mid_recv.at[part, j - 1, k, o])
+            elif part == 0:
+                wait(full.at[g, :, pair(k)[0], zl, 1 - y], y_send, y_recv.at[k])
+            last(j, k, o, part)
+
+    def onward(j, k, o):
         for part in range(2):
             way = j % 2
-            came = block(part, froms[j], 1 - 2 * way, o)
-            wait(came, last_send, last_recv.at[part, j, o])
+            came = block(part, froms[j], 1 - 2 * way, k, o)
+            wait(came, last_send, last_recv.at[part, j, k, o])
             copy(came, end_send, end_recv, hop(1 - part, 1 - 2 * way)).start()
 
-    for dy in range(2):
-        if dy:
-            here = full.at[g, :, zl, y]
-            copy(here, y_send, y_recv, device(0, 1, 0, 0)).start()
-        for j, d in enumerate(AROUND):
-            for part in range(2):
-                copy(block(part, 0, 0, 0), mid_send, mid_recv.at[part, j, dy], hop(part, d, dy)).start()
-    for part in range(2):
-        last(part, 0, 0)
+    finish(0)
     moved = momentum_rate * momentum[...]
-    own = grad.at[zh]
+    own = rows_of(grad, 0)
     for i in range(2):
         new_momentum[i * half : (i + 1) * half] = moved[i * half : (i + 1) * half] + own[i]
         new_master[i * half : (i + 1) * half] = mine[i] - outer_rate * (1 + momentum_rate) * own[i]
-    for j in range(1, 4):
-        middle(j, 0)
-    wait(full.at[g, :, zl, 1 - y], y_send, y_recv)
-    for part in range(2):
-        last(part, 0, 1)
-    for j in range(1, 4):
-        middle(j, 1)
+    for j, k, o in ((1, 0, 0), (2, 0, 0), (0, 0, 1)):
+        middle(j, k, o)
+    onward(0, 0, 0)
+    middle(3, 0, 0)
+    middle(1, 0, 1)
+    for way in range(2):
+        far(way, 2, rows_of(base, 2).at[way]).wait_recv()
+    finish(1)
+    onward(1, 0, 0)
+    onward(2, 0, 0)
+    middle(2, 0, 1)
+    onward(0, 0, 1)
+    middle(3, 0, 1)
+    onward(3, 0, 0)
+    onward(1, 0, 1)
+    for j, k, o in ((1, 1, 0), (2, 1, 0), (0, 1, 1)):
+        middle(j, k, o)
+    onward(0, 1, 0)
+    onward(2, 0, 1)
+    middle(1, 1, 1)
+    middle(2, 1, 1)
+    onward(3, 0, 1)
+    middle(3, 1, 0)
+    onward(2, 1, 0)
+    onward(1, 1, 0)
+    onward(0, 1, 1)
+    middle(3, 1, 1)
+    onward(1, 1, 1)
+    onward(2, 1, 1)
+    onward(3, 1, 0)
+    onward(3, 1, 1)
     wait_sent(incoming, sum_send)
-    wait_sent(base.at[0:3], far_send)
-    wait_sent(full.at[0, :, 0, 0], y_send)
-    for o in range(2):
-        for j in range(4):
-            onward(j, o)
-    wait_sent(full.at[0:3, :, 0], mid_send)
+    wait_sent(incoming.at[0:6], far_send)
+    wait_sent(full.at[0, :, :, 0, 0], y_send)
+    wait_sent(full.at[0:3, :, :, 0], mid_send)
     wait_sent(full.at[0:2], last_send)
     wait(full.at[0:2], end_send, end_recv)
     wait_sent(full.at[0:1], end_send)
@@ -194,8 +238,8 @@
     vmem = pl.BlockSpec(memory_space=pltpu.VMEM)
     dma = pltpu.SemaphoreType.DMA
     zls = depth // 4
-    full = (groups, 4, zls, 2, 2, rows // 2, cols)
-    four = (4, 2, rows // 2, cols)
+    full = (groups, 2, 2, zls, 2, 2, rows // 2, cols)
+    four = (2, 2, 2, rows // 2, cols)
     results = pl.pallas_call(
         kernel,
         out_shape=(
@@ -214,8 +258,8 @@
             pltpu.VMEM((groups * tensors - 1, 2 * rows, 2 * rank), jnp.float32),
             pltpu.VMEM(four, jnp.float32),
             pltpu.VMEM(four, jnp.float32),
-            dma((4,)), dma, dma, dma, dma((4,)), dma, dma,
-            dma, dma((2, 3, 2)), dma, dma((2, 4, 2)), dma, dma,
+            dma((4,)), dma, dma, dma, dma((2, 3)), dma, dma((2,)),
+            dma, dma((2, 3, 2, 2)), dma, dma((2, 4, 2, 2)), dma, dma,
         ],
         compiler_params=pltpu.CompilerParams(collective_id=0, has_side_effects=True),
     )(deltas.reshape(groups, 4, zls, 2, rows, cols), factor.T, master, momentum)

time: 42.2 us -> 42.5 us (level)
  the two profiles are of different devices: /device:TPU:6 before, /device:TPU:4 now
where the time goes in v5:
time: 42.5 us; the launch traced here: 42.3 us
  Pallas kernels  41.7 us (98%)
  between operations  0.64 us (2%)
    pallas_call x1, Pallas kernels, shards(): pl.pallas_call(kernel, out_shape=(pltpu.VMEM(master.shape, jnp.float32),...  40.3 us
    pallas_call x1, Pallas kernels, shards(): pl.pallas_call(store, out_shape=tuple((jax.ShapeDtypeStruct(r.shape, r.dt...  1.37 us

profile of v5, /device:TPU:4, one launch (start us, length us, event | category | flops | bytes accessed | tf_op | source)
XLA Modules:
  0.0 42.3 jit_solution(11476883449906472478)
XLA Ops:
  0.6 40.3 %shard_map.67 = (f32[16,512]{1,0:T(8,128)S(1)}, f32[16,512]{1,0:T(8,128)S(1)}, bf16[4,2,2,4,2,2,8,512]{7,6,5,4,3,2,1,0:T(8,128)(2,1)S(1)}) custom-call(bf16[4,4,4,2,16,512]{5,4,3,2,1,0:T(8,128)(2,1)} %bitcast.3, bf16[64,512]{1,0:T(8,128)(2,1)} %bitcast.4, f32[16,512]{1,0:T(8,128)} %master_ref.1, f32[16,512]{1,0:T(8,128)} %momentum_ref.1), custom_call_target="tpu_custom_call" | custom-call | tf_op jit(solution)/shard_map/pallas_call | solution.py:243
  41.0 1.4 %shard_map.68 = (f32[16,512]{1,0:T(8,128)}, f32[16,512]{1,0:T(8,128)}, bf16[4,2,2,4,2,2,8,512]{7,6,5,4,3,2,1,0:T(8,128)(2,1)}) custom-call(f32[16,512]{1,0:T(8,128)S(1)} %get-tuple-element.9.refs_0_, f32[16,512]{1,0:T(8,128)S(1)} %get-tuple-element.10.refs_1_, bf16[4,2,2,4,2,2,8,512]{7,6,5,4,3,2,1,0:T(8,128)(2,1)S(1)} %get-tuple-element.11.refs_2_), custom_call_target="tpu_custom_call" | custom-call | tf_op jit(solution)/shard_map/pallas_call | solution.py:266

commit v6 on v5

--- a/solution.py
+++ b/solution.py
@@ -178,37 +178,25 @@
     for i in range(2):
         new_momentum[i * half : (i + 1) * half] = moved[i * half : (i + 1) * half] + own[i]
         new_master[i * half : (i + 1) * half] = mine[i] - outer_rate * (1 + momentum_rate) * own[i]
-    for j, k, o in ((1, 0, 0), (2, 0, 0), (0, 0, 1)):
-        middle(j, k, o)
-    onward(0, 0, 0)
-    middle(3, 0, 0)
-    middle(1, 0, 1)
     for way in range(2):
         far(way, 2, rows_of(base, 2).at[way]).wait_recv()
     finish(1)
-    onward(1, 0, 0)
-    onward(2, 0, 0)
-    middle(2, 0, 1)
-    onward(0, 0, 1)
-    middle(3, 0, 1)
-    onward(3, 0, 0)
-    onward(1, 0, 1)
-    for j, k, o in ((1, 1, 0), (2, 1, 0), (0, 1, 1)):
-        middle(j, k, o)
-    onward(0, 1, 0)
-    onward(2, 0, 1)
-    middle(1, 1, 1)
-    middle(2, 1, 1)
-    onward(3, 0, 1)
-    middle(3, 1, 0)
-    onward(2, 1, 0)
-    onward(1, 1, 0)
-    onward(0, 1, 1)
-    middle(3, 1, 1)
-    onward(1, 1, 1)
-    onward(2, 1, 1)
-    onward(3, 1, 0)
-    onward(3, 1, 1)
+    for j in (1, 2, 3):
+        middle(j, 0, 0)
+    for j in range(4):
+        middle(j, 0, 1)
+    for j in (1, 2, 3):
+        middle(j, 1, 0)
+    for j in range(4):
+        middle(j, 1, 1)
+    for j in range(4):
+        onward(j, 0, 0)
+    for j in range(4):
+        onward(j, 0, 1)
+    for j in range(4):
+        onward(j, 1, 0)
+    for j in range(4):
+        onward(j, 1, 1)
     wait_sent(incoming, sum_send)
     wait_sent(incoming.at[0:6], far_send)
     wait_sent(full.at[0, :, :, 0, 0], y_send)

time: 42.5 us -> 40.2 us (0.946)
  the two profiles are of different devices: /device:TPU:4 before, /device:TPU:32 now
where the time goes in v6:
time: 40.2 us; the launch traced here: 40.1 us
  Pallas kernels  39.4 us (98%)
  between operations  0.64 us (2%)
    pallas_call x1, Pallas kernels, shards(): pl.pallas_call(kernel, out_shape=(pltpu.VMEM(master.shape, jnp.float32),...  38 us
    pallas_call x1, Pallas kernels, shards(): pl.pallas_call(store, out_shape=tuple((jax.ShapeDtypeStruct(r.shape, r.dt...  1.37 us

profile of v6, /device:TPU:32, one launch (start us, length us, event | category | flops | bytes accessed | tf_op | source)
XLA Modules:
  0.0 40.1 jit_solution(1834720427584295986)
XLA Ops:
  0.6 38.0 %shard_map.67 = (f32[16,512]{1,0:T(8,128)S(1)}, f32[16,512]{1,0:T(8,128)S(1)}, bf16[4,2,2,4,2,2,8,512]{7,6,5,4,3,2,1,0:T(8,128)(2,1)S(1)}) custom-call(bf16[4,4,4,2,16,512]{5,4,3,2,1,0:T(8,128)(2,1)} %bitcast.3, bf16[64,512]{1,0:T(8,128)(2,1)} %bitcast.4, f32[16,512]{1,0:T(8,128)} %master_ref.1, f32[16,512]{1,0:T(8,128)} %momentum_ref.1), custom_call_target="tpu_custom_call" | custom-call | tf_op jit(solution)/shard_map/pallas_call | solution.py:231
  38.7 1.4 %shard_map.68 = (f32[16,512]{1,0:T(8,128)}, f32[16,512]{1,0:T(8,128)}, bf16[4,2,2,4,2,2,8,512]{7,6,5,4,3,2,1,0:T(8,128)(2,1)}) custom-call(f32[16,512]{1,0:T(8,128)S(1)} %get-tuple-element.9.refs_0_, f32[16,512]{1,0:T(8,128)S(1)} %get-tuple-element.10.refs_1_, bf16[4,2,2,4,2,2,8,512]{7,6,5,4,3,2,1,0:T(8,128)(2,1)S(1)} %get-tuple-element.11.refs_2_), custom_call_target="tpu_custom_call" | custom-call | tf_op jit(solution)/shard_map/pallas_call | solution.py:254

commit v7 on v6

--- a/solution.py
+++ b/solution.py
@@ -108,9 +108,6 @@
         came = rows_of(base, 2 * way - 1).at[way]
         far(way, 0, came).wait_recv()
         far(way, 2, came).start()
-    for way in range(2):
-        far(way, 1, rows_of(base, 2 * way - 1).at[1 - way]).wait_recv()
-
     wait(incoming, sum_send, sum_recv)
     total = partial[g]
     for i in range(len(sums)):
@@ -121,56 +118,66 @@
         precision=lax.Precision.HIGHEST, preferred_element_type=jnp.float32,
     ) / groups
     grad[...] = outer_grad.reshape(grad.shape)
-
-    def pair(k, dz=0):
+    for way in range(2):
+        far(way, 1, rows_of(base, 2 * way - 1).at[1 - way]).wait_recv()
+
+    def spots(k, dz, index):
         zh_of, zl_of = place(dz)
-        return (zh_of + 1 - k) % 2, zl_of
+        far_of = around(zh_of, 2, zhs)
+        single = zh_of if k == 0 else far_of
+        found = [full.at[(index[0], single // 2, single % 2, zl_of) + index[1:]]]
+        if k == 0:
+            found.append(full.at[(index[0], slice(None), 1 - zh_of % 2, zl_of) + index[1:]])
+        return found
+
+    def amount(k, *index):
+        return full.at[(0, 0, 0, slice(0, 3) if k == 0 else 0) + index]
 
     def hop(axis, d, dy=0):
         return device(d, dy, 0, 0) if axis == 0 else device(0, dy, d, 0)
 
     def block(part, u, w, k, o):
         dg, dz = (u, w) if part == 0 else (w, u)
-        parity, zl_of = pair(k, -dz)
-        return full.at[around(g, -dg, groups), :, parity, zl_of, y if o == 0 else 1 - y, part]
+        return spots(k, -dz, (around(g, -dg, groups), y if o == 0 else 1 - y, part))
 
     froms = (0,) + AROUND
 
     def last(j, k, o, part):
         for way in range(2):
             came = last_recv.at[part, j, k, o] if j % 2 == way else end_recv
-            copy(block(part, froms[j], 0, k, o), last_send, came, hop(1 - part, 1 - 2 * way)).start()
+            for piece in block(part, froms[j], 0, k, o):
+                copy(piece, last_send, came, hop(1 - part, 1 - 2 * way)).start()
 
     def finish(k):
-        parity = pair(k)[0]
-        fresh = base[:, parity] - outer_rate * (1 + momentum_rate) * grad[:, parity]
-        full[g, :, parity, zl, y] = fresh.astype(jnp.bfloat16)
+        for step in (0, 1, -1) if k == 0 else (2,):
+            other = around(zh, step, zhs)
+            fresh = rows_of(base, step)[...] - outer_rate * (1 + momentum_rate) * rows_of(grad, step)[...]
+            full[g, other // 2, other % 2, zl, y] = fresh.astype(jnp.bfloat16)
         for dy in range(2):
             if dy:
-                here = full.at[g, :, parity, zl, y]
-                copy(here, y_send, y_recv.at[k], device(0, 1, 0, 0)).start()
+                for piece in spots(k, 0, (g, y)):
+                    copy(piece, y_send, y_recv.at[k], device(0, 1, 0, 0)).start()
             for j, d in enumerate(AROUND):
                 for part in range(2):
-                    copy(
-                        block(part, 0, 0, k, 0), mid_send, mid_recv.at[part, j, k, dy], hop(part, d, dy)
-                    ).start()
+                    for piece in block(part, 0, 0, k, 0):
+                        copy(piece, mid_send, mid_recv.at[part, j, k, dy], hop(part, d, dy)).start()
         for part in range(2):
             last(0, k, 0, part)
 
     def middle(j, k, o):
         for part in range(2):
             if j:
-                wait(block(part, froms[j], 0, k, o), mid_send, mid_recv.at[part, j - 1, k, o])
+                wait(amount(k, 0, 0), mid_send, mid_recv.at[part, j - 1, k, o])
             elif part == 0:
-                wait(full.at[g, :, pair(k)[0], zl, 1 - y], y_send, y_recv.at[k])
+                wait(amount(k, 0), y_send, y_recv.at[k])
             last(j, k, o, part)
 
     def onward(j, k, o):
         for part in range(2):
             way = j % 2
-            came = block(part, froms[j], 1 - 2 * way, k, o)
-            wait(came, last_send, last_recv.at[part, j, k, o])
-            copy(came, end_send, end_recv, hop(1 - part, 1 - 2 * way)).start()
+            wait(amount(k, 0, 0), last_send, last_recv.at[part, j, k, o])
+            for piece in block(part, froms[j], 1 - 2 * way, k, o):
+                copy(piece, end_send, end_recv, hop(1 - part, 1 - 2 * way)).start()
 
     finish(0)
     moved = momentum_rate * momentum[...]

time: 40.2 us -> 39.9 us (level)
  the two profiles are of different devices: /device:TPU:32 before, /device:TPU:6 now
where the time goes in v7:
time: 39.9 us; the launch traced here: 39.2 us
  Pallas kernels  38.5 us (96%)
  between operations  0.64 us (2%)
    pallas_call x1, Pallas kernels, shards(): pl.pallas_call(kernel, out_shape=(pltpu.VMEM(master.shape, jnp.float32),...  37.1 us
    pallas_call x1, Pallas kernels, shards(): pl.pallas_call(store, out_shape=tuple((jax.ShapeDtypeStruct(r.shape, r.dt...  1.37 us

profile of v7, /device:TPU:6, one launch (start us, length us, event | category | flops | bytes accessed | tf_op | source)
XLA Modules:
  0.0 39.2 jit_solution(4453936314655396677)
XLA Ops:
  0.6 37.1 %shard_map.67 = (f32[16,512]{1,0:T(8,128)S(1)}, f32[16,512]{1,0:T(8,128)S(1)}, bf16[4,2,2,4,2,2,8,512]{7,6,5,4,3,2,1,0:T(8,128)(2,1)S(1)}) custom-call(bf16[4,4,4,2,16,512]{5,4,3,2,1,0:T(8,128)(2,1)} %bitcast.3, bf16[64,512]{1,0:T(8,128)(2,1)} %bitcast.4, f32[16,512]{1,0:T(8,128)} %master_ref.1, f32[16,512]{1,0:T(8,128)} %momentum_ref.1), custom_call_target="tpu_custom_call" | custom-call | tf_op jit(solution)/shard_map/pallas_call | solution.py:238
  37.8 1.4 %shard_map.68 = (f32[16,512]{1,0:T(8,128)}, f32[16,512]{1,0:T(8,128)}, bf16[4,2,2,4,2,2,8,512]{7,6,5,4,3,2,1,0:T(8,128)(2,1)}) custom-call(f32[16,512]{1,0:T(8,128)S(1)} %get-tuple-element.9.refs_0_, f32[16,512]{1,0:T(8,128)S(1)} %get-tuple-element.10.refs_1_, bf16[4,2,2,4,2,2,8,512]{7,6,5,4,3,2,1,0:T(8,128)(2,1)S(1)} %get-tuple-element.11.refs_2_), custom_call_target="tpu_custom_call" | custom-call | tf_op jit(solution)/shard_map/pallas_call | solution.py:261

commit v8 on v7

--- a/solution.py
+++ b/solution.py
@@ -46,17 +46,17 @@
         pltpu.make_async_copy(deltas_ref.at[:, :, zl, y], delta, in_sem.at[2]),
         pltpu.make_async_copy(factor_ref, factor, in_sem.at[3]),
     ]
-    for load in loads:
-        load.start()
-
     sums = [(dg, dt) for dg in (2, 1, -1, 0) for dt in (2, 1, -1, 0) if dg or dt]
     peers = [(0, 0, dz, 0) for dz in (zls, -zls)]
     peers += [(0, dy, dz, 0) for dz in (2, -2, 1, -1) for dy in range(2)]
     peers += [(dg, 1, 0, 0) for dg in (2, 1, -1, 0)]
     peers += [(dg, 0, 0, dt) for dg, dt in sums]
     barrier = pltpu.get_barrier_semaphore()
-    for peer in peers:
+    for i, peer in enumerate(peers):
         pl.semaphore_signal(barrier, inc=1, device_id=device(*peer), device_id_type=MESH)
+        if i == 1:
+            for load in loads:
+                load.start()
 
     loads[0].wait()
     loads[1].wait()
@@ -118,8 +118,6 @@
         precision=lax.Precision.HIGHEST, preferred_element_type=jnp.float32,
     ) / groups
     grad[...] = outer_grad.reshape(grad.shape)
-    for way in range(2):
-        far(way, 1, rows_of(base, 2 * way - 1).at[1 - way]).wait_recv()
 
     def spots(k, dz, index):
         zh_of, zl_of = place(dz)
@@ -142,27 +140,27 @@
 
     froms = (0,) + AROUND
 
-    def last(j, k, o, part):
+    def last(j, k, o, part, picked=slice(None)):
         for way in range(2):
             came = last_recv.at[part, j, k, o] if j % 2 == way else end_recv
-            for piece in block(part, froms[j], 0, k, o):
+            for piece in block(part, froms[j], 0, k, o)[picked]:
                 copy(piece, last_send, came, hop(1 - part, 1 - 2 * way)).start()
 
-    def finish(k):
-        for step in (0, 1, -1) if k == 0 else (2,):
+    def finish(k, steps, picked):
+        for step in steps:
             other = around(zh, step, zhs)
             fresh = rows_of(base, step)[...] - outer_rate * (1 + momentum_rate) * rows_of(grad, step)[...]
             full[g, other // 2, other % 2, zl, y] = fresh.astype(jnp.bfloat16)
         for dy in range(2):
             if dy:
-                for piece in spots(k, 0, (g, y)):
+                for piece in spots(k, 0, (g, y))[picked]:
                     copy(piece, y_send, y_recv.at[k], device(0, 1, 0, 0)).start()
             for j, d in enumerate(AROUND):
                 for part in range(2):
-                    for piece in block(part, 0, 0, k, 0):
+                    for piece in block(part, 0, 0, k, 0)[picked]:
                         copy(piece, mid_send, mid_recv.at[part, j, k, dy], hop(part, d, dy)).start()
         for part in range(2):
-            last(0, k, 0, part)
+            last(0, k, 0, part, picked)
 
     def middle(j, k, o):
         for part in range(2):
@@ -179,7 +177,10 @@
             for piece in block(part, froms[j], 1 - 2 * way, k, o):
                 copy(piece, end_send, end_recv, hop(1 - part, 1 - 2 * way)).start()
 
-    finish(0)
+    finish(0, (0,), slice(0, 1))
+    for way in range(2):
+        far(way, 1, rows_of(base, 2 * way - 1).at[1 - way]).wait_recv()
+    finish(0, (1, -1), slice(1, 2))
     moved = momentum_rate * momentum[...]
     own = rows_of(grad, 0)
     for i in range(2):
@@ -187,7 +188,7 @@
         new_master[i * half : (i + 1) * half] = mine[i] - outer_rate * (1 + momentum_rate) * own[i]
     for way in range(2):
         far(way, 2, rows_of(base, 2).at[way]).wait_recv()
-    finish(1)
+    finish(1, (2,), slice(0, 1))
     for j in (1, 2, 3):
         middle(j, 0, 0)
     for j in range(4):
@@ -216,7 +217,9 @@
 def store(*refs):
     sem = refs[-1]
     count = len(refs) // 2
-    moves = [pltpu.make_async_copy(refs[i], refs[count + i], sem.at[i]) for i in range(count)]
+    moves = [pltpu.make_async_copy(refs[i], refs[count + i], sem.at[i]) for i in range(count - 1)]
+    for i in range(refs[count - 1].shape[0]):
+        moves.append(pltpu.make_async_copy(refs[count - 1].at[i], refs[-2].at[i], sem.at[count - 1 + i]))
     for move in moves:
         move.start()
     for move in moves:
@@ -263,7 +266,7 @@
         out_shape=tuple(jax.ShapeDtypeStruct(r.shape, r.dtype) for r in results),
         in_specs=[anywhere] * 3,
         out_specs=(anywhere,) * 3,
-        scratch_shapes=[dma((3,))],
+        scratch_shapes=[dma((2 + groups,))],
         compiler_params=pltpu.CompilerParams(vmem_limit_bytes=1 << 20),
     )(*results)
     return new_master, new_momentum, weights.reshape(groups * depth * 2 * rows, cols)

time: 39.9 us -> 40.1 us (level)
  the two profiles are of different devices: /device:TPU:6 before, /device:TPU:32 now
where the time goes in v8:
time: 40.1 us; the launch traced here: 40 us
  Pallas kernels  39.4 us (98%)
  between operations  0.64 us (2%)
    pallas_call x1, Pallas kernels, shards(): pl.pallas_call(kernel, out_shape=(pltpu.VMEM(master.shape, jnp.float32),...  38 us
    pallas_call x1, Pallas kernels, shards(): pl.pallas_call(store, out_shape=tuple((jax.ShapeDtypeStruct(r.shape, r.dt...  1.39 us

profile of v8, /device:TPU:32, one launch (start us, length us, event | category | flops | bytes accessed | tf_op | source)
XLA Modules:
  0.0 40.0 jit_solution(4487566996145923307)
XLA Ops:
  0.6 38.0 %shard_map.67 = (f32[16,512]{1,0:T(8,128)S(1)}, f32[16,512]{1,0:T(8,128)S(1)}, bf16[4,2,2,4,2,2,8,512]{7,6,5,4,3,2,1,0:T(8,128)(2,1)S(1)}) custom-call(bf16[4,4,4,2,16,512]{5,4,3,2,1,0:T(8,128)(2,1)} %bitcast.3, bf16[64,512]{1,0:T(8,128)(2,1)} %bitcast.4, f32[16,512]{1,0:T(8,128)} %master_ref.1, f32[16,512]{1,0:T(8,128)} %momentum_ref.1), custom_call_target="tpu_custom_call" | custom-call | tf_op jit(solution)/shard_map/pallas_call | solution.py:241
  38.6 1.4 %shard_map.68 = (f32[16,512]{1,0:T(8,128)}, f32[16,512]{1,0:T(8,128)}, bf16[4,2,2,4,2,2,8,512]{7,6,5,4,3,2,1,0:T(8,128)(2,1)}) custom-call(f32[16,512]{1,0:T(8,128)S(1)} %get-tuple-element.9.refs_0_, f32[16,512]{1,0:T(8,128)S(1)} %get-tuple-element.10.refs_1_, bf16[4,2,2,4,2,2,8,512]{7,6,5,4,3,2,1,0:T(8,128)(2,1)S(1)} %get-tuple-element.11.refs_2_), custom_call_target="tpu_custom_call" | custom-call | tf_op jit(solution)/shard_map/pallas_call | solution.py:264

commit v9 on v8

--- a/solution.py
+++ b/solution.py
@@ -46,17 +46,17 @@
         pltpu.make_async_copy(deltas_ref.at[:, :, zl, y], delta, in_sem.at[2]),
         pltpu.make_async_copy(factor_ref, factor, in_sem.at[3]),
     ]
+    for load in loads:
+        load.start()
+
     sums = [(dg, dt) for dg in (2, 1, -1, 0) for dt in (2, 1, -1, 0) if dg or dt]
     peers = [(0, 0, dz, 0) for dz in (zls, -zls)]
     peers += [(0, dy, dz, 0) for dz in (2, -2, 1, -1) for dy in range(2)]
     peers += [(dg, 1, 0, 0) for dg in (2, 1, -1, 0)]
     peers += [(dg, 0, 0, dt) for dg, dt in sums]
     barrier = pltpu.get_barrier_semaphore()
-    for i, peer in enumerate(peers):
+    for peer in peers:
         pl.semaphore_signal(barrier, inc=1, device_id=device(*peer), device_id_type=MESH)
-        if i == 1:
-            for load in loads:
-                load.start()
 
     loads[0].wait()
     loads[1].wait()
@@ -217,9 +217,7 @@
 def store(*refs):
     sem = refs[-1]
     count = len(refs) // 2
-    moves = [pltpu.make_async_copy(refs[i], refs[count + i], sem.at[i]) for i in range(count - 1)]
-    for i in range(refs[count - 1].shape[0]):
-        moves.append(pltpu.make_async_copy(refs[count - 1].at[i], refs[-2].at[i], sem.at[count - 1 + i]))
+    moves = [pltpu.make_async_copy(refs[i], refs[count + i], sem.at[i]) for i in range(count)]
     for move in moves:
         move.start()
     for move in moves:
@@ -266,7 +264,7 @@
         out_shape=tuple(jax.ShapeDtypeStruct(r.shape, r.dtype) for r in results),
         in_specs=[anywhere] * 3,
         out_specs=(anywhere,) * 3,
-        scratch_shapes=[dma((2 + groups,))],
+        scratch_shapes=[dma((3,))],
         compiler_params=pltpu.CompilerParams(vmem_limit_bytes=1 << 20),
     )(*results)
     return new_master, new_momentum, weights.reshape(groups * depth * 2 * rows, cols)

time: 40.1 us -> 40.1 us (level)
  no operation moved by 1% of the time
where the time goes in v9:
time: 40.1 us; the launch traced here: 40 us
  Pallas kernels  39.3 us (98%)
  between operations  0.64 us (2%)
    pallas_call x1, Pallas kernels, shards(): pl.pallas_call(kernel, out_shape=(pltpu.VMEM(master.shape, jnp.float32),...  38 us
    pallas_call x1, Pallas kernels, shards(): pl.pallas_call(store, out_shape=tuple((jax.ShapeDtypeStruct(r.shape, r.dt...  1.37 us

profile of v9, /device:TPU:32, one launch (start us, length us, event | category | flops | bytes accessed | tf_op | source)
XLA Modules:
  0.0 40.0 jit_solution(2535478913783195214)
XLA Ops:
  0.6 38.0 %shard_map.67 = (f32[16,512]{1,0:T(8,128)S(1)}, f32[16,512]{1,0:T(8,128)S(1)}, bf16[4,2,2,4,2,2,8,512]{7,6,5,4,3,2,1,0:T(8,128)(2,1)S(1)}) custom-call(bf16[4,4,4,2,16,512]{5,4,3,2,1,0:T(8,128)(2,1)} %bitcast.3, bf16[64,512]{1,0:T(8,128)(2,1)} %bitcast.4, f32[16,512]{1,0:T(8,128)} %master_ref.1, f32[16,512]{1,0:T(8,128)} %momentum_ref.1), custom_call_target="tpu_custom_call" | custom-call | tf_op jit(solution)/shard_map/pallas_call | solution.py:239
  38.6 1.4 %shard_map.68 = (f32[16,512]{1,0:T(8,128)}, f32[16,512]{1,0:T(8,128)}, bf16[4,2,2,4,2,2,8,512]{7,6,5,4,3,2,1,0:T(8,128)(2,1)}) custom-call(f32[16,512]{1,0:T(8,128)S(1)} %get-tuple-element.9.refs_0_, f32[16,512]{1,0:T(8,128)S(1)} %get-tuple-element.10.refs_1_, bf16[4,2,2,4,2,2,8,512]{7,6,5,4,3,2,1,0:T(8,128)(2,1)S(1)} %get-tuple-element.11.refs_2_), custom_call_target="tpu_custom_call" | custom-call | tf_op jit(solution)/shard_map/pallas_call | solution.py:262
